TPU v7x, 32 devices: a whole 2x2x4 slice. The times are simulated.
32 devices in a mesh: dp: 8 (over z, y), tensor: 4 (over x, core).
Axes of the slice: x: 2, y: 2, z: 4, core: 2. Of those that a mesh axis runs over, the one named last changes fastest.
Arguments:
- tokens: bfloat16 [8192, 1024], P(('dp', 'tensor')), may hold values from -16 to 16
- cotangent: bfloat16 [8192, 1024], P(('dp', 'tensor')), may hold values from -16 to 16
- gain_attn: float32 [1024], replicated, may hold values from 0.1 to 1.9
- bias_attn: float32 [1024], replicated, may hold values from -1.75 to 1.75
- gain_mlp: float32 [1024], replicated, may hold values from 0.1 to 1.9
- bias_mlp: float32 [1024], replicated, may hold values from -1.75 to 1.75
- qkv_weight: bfloat16 [1024, 3072], P(None, 'tensor'), may hold values from -0.1875 to 0.1875
- qkv_bias: float32 [3072], P('tensor'), may hold values from -1.75 to 1.75
- out_weight: bfloat16 [1024, 1024], P('tensor'), may hold values from -2.5 to 2.5
- out_bias: float32 [1024], replicated, may hold values from -1.75 to 1.75
- up_weight: bfloat16 [1024, 4096], P(None, 'tensor'), may hold values from -0.1875 to 0.1875
- up_bias: float32 [4096], P('tensor'), may hold values from -1.75 to 1.75
- down_weight: bfloat16 [4096, 1024], P('tensor'), may hold values from -0.09375 to 0.09375
- down_bias: float32 [1024], replicated, may hold values from -1.75 to 1.75
Outputs:
- mixed: bfloat16 [8192, 1024], P(('dp', 'tensor'))
- input_grad: float32 [8192, 1024], P(('dp', 'tensor'))
- gain_attn_grad: float32 [1024], replicated
- bias_attn_grad: float32 [1024], replicated
- gain_mlp_grad: float32 [1024], replicated
- bias_mlp_grad: float32 [1024], replicated
- qkv_weight_grad: float32 [1024, 3072], P(None, 'tensor')
- qkv_bias_grad: float32 [3072], P('tensor')
- out_weight_grad: float32 [1024, 1024], P('tensor')
- out_bias_grad: float32 [1024], replicated
- up_weight_grad: float32 [1024, 4096], P(None, 'tensor')
- up_bias_grad: float32 [4096], P('tensor')
- down_weight_grad: float32 [4096, 1024], P('tensor')
- down_bias_grad: float32 [1024], replicated
- statistics: float32 [3], replicated
All inputs are finite; a program needn't handle non-finite values.
Results may differ from a plain program's by a relative error of at most 0.012.
The roundings to bfloat16 on the way count: a program that leaves them out, or rounds other values in their place, can miss the bound.
Values may be sent and summed in bfloat16 or wider, within the bound.
A program may use at most 192 MiB of HBM per device.

v0:
```python
import math
import jax
import jax.numpy as jnp
from jax import lax
from jax.sharding import PartitionSpec as P

HD = 64
ROT = 16
epsilon = 1e-05


def angle_tables(seq_len):
    positions = jnp.arange(seq_len, dtype=jnp.float32)
    inverse = 10000.0 ** (-(jnp.arange(ROT // 2, dtype=jnp.float32) * 2.0 / ROT))
    angles = positions[:, None] * inverse[None, :]
    cosine = jnp.concatenate([jnp.cos(angles), jnp.cos(angles)], axis=-1)[:, None, :]
    sine_part = jnp.concatenate([jnp.sin(angles), jnp.sin(angles)], axis=-1)[:, None, :]
    return (cosine, sine_part)


def rotate(field_in, cosine, sine_part):
    half_rot = ROT // 2
    first_half = field_in[..., :half_rot]
    second = field_in[..., half_rot:ROT]
    turned = jnp.concatenate([-second, first_half], axis=-1)
    return jnp.concatenate(
        [field_in[..., :ROT] * cosine + turned * sine_part, field_in[..., ROT:]], axis=-1
    )


def unrotate(grad_in, cosine, sine_part):
    half_rot = ROT // 2
    head_part = grad_in[..., :ROT]
    scaled = head_part * sine_part
    turned = jnp.concatenate([scaled[..., half_rot:], -scaled[..., :half_rot]], axis=-1)
    return jnp.concatenate([head_part * cosine + turned, grad_in[..., ROT:]], axis=-1)


def normalize(raw_rows):
    average = jnp.mean(raw_rows, axis=-1, keepdims=True)
    centred = raw_rows - average
    spread = jnp.mean(centred * centred, axis=-1, keepdims=True)
    inverse_root = lax.rsqrt(spread + epsilon)
    return (centred * inverse_root, inverse_root)


def against(left, right):
    return lax.dot_general(
        left, right, (((1,), (1,)), ((), ())), preferred_element_type=jnp.float32
    )


def per_device(
    tokens,
    cotangent,
    gain_attn,
    bias_attn,
    gain_mlp,
    bias_mlp,
    qkv_weight,
    qkv_bias,
    out_weight,
    out_bias,
    up_weight,
    up_bias,
    down_weight,
    down_bias,
):
    own_rows = tokens.shape[0]
    model_width = tokens.shape[1]
    heads_here = out_weight.shape[0] // HD
    score_scale = HD ** (-0.5)
    whole_rows = lax.all_gather(tokens, "tensor", axis=0, tiled=True)
    seq_len = whole_rows.shape[0]
    normed, _ = normalize(whole_rows.astype(jnp.float32))
    attention_input = (normed * gain_attn + bias_attn).astype(jnp.bfloat16)
    feed_input = (normed * gain_mlp + bias_mlp).astype(jnp.bfloat16)
    projected = jnp.dot(attention_input, qkv_weight, preferred_element_type=jnp.float32) + qkv_bias
    projected = projected.reshape(seq_len, heads_here, 3, HD)
    cosine, sine_part = angle_tables(seq_len)
    queries = rotate(projected[:, :, 0], cosine, sine_part).astype(jnp.bfloat16)
    keys_all = rotate(projected[:, :, 1], cosine, sine_part).astype(jnp.bfloat16)
    values_all = projected[:, :, 2].astype(jnp.bfloat16)
    preact = jnp.dot(feed_input, up_weight, preferred_element_type=jnp.float32) + up_bias
    hidden = jax.nn.gelu(preact, approximate=False).astype(jnp.bfloat16)
    block_rows = min(512, seq_len)
    block_total = seq_len // block_rows
    key_positions = jnp.arange(seq_len, dtype=jnp.int32)

    def causal_mask(offset):
        return key_positions[None, :] <= (offset + jnp.arange(block_rows, dtype=jnp.int32))[:, None]

    def forward_block(number):
        offset = number * block_rows
        query_rows = lax.dynamic_slice_in_dim(queries, offset, block_rows, 0)
        scores = (
            jnp.einsum("qhd,khd->hqk", query_rows, keys_all, preferred_element_type=jnp.float32)
            * score_scale
        )
        scores = jnp.where(causal_mask(offset)[None], scores, -1e30)
        highest = jnp.max(scores, axis=-1, keepdims=True)
        weights = jnp.exp(scores - highest)
        totals = jnp.sum(weights, axis=-1, keepdims=True)
        soft_rows = (weights / totals).astype(jnp.bfloat16)
        context_rows = jnp.einsum(
            "hqk,khd->qhd", soft_rows, values_all, preferred_element_type=jnp.float32
        ).astype(jnp.bfloat16)
        log_totals = (highest + jnp.log(totals))[:, :, 0].T
        return (context_rows, log_totals)

    context_blocks, log_blocks = lax.map(forward_block, jnp.arange(block_total, dtype=jnp.int32))
    context = context_blocks.reshape(seq_len, heads_here * HD)
    log_sums = log_blocks.reshape(seq_len, heads_here)
    context_rows = context
    branch = lax.psum_scatter(
        jnp.dot(context_rows, out_weight, preferred_element_type=jnp.float32)
        + jnp.dot(hidden, down_weight, preferred_element_type=jnp.float32),
        "tensor",
        scatter_dimension=0,
        tiled=True,
    )
    branch = branch + out_bias + down_bias
    residual_out = tokens.astype(jnp.float32) + branch
    mixed_out = residual_out.astype(jnp.bfloat16)
    forward_squares = jnp.stack([jnp.sum(residual_out * residual_out), jnp.sum(branch * branch)])
    forward_totals = lax.psum(forward_squares, ("dp", "tensor"))
    upstream = lax.all_gather(cotangent, "tensor", axis=0, tiled=True)
    out_weight_grad = jnp.einsum("sa,sd->ad", context, upstream, preferred_element_type=jnp.float32)
    down_weight_grad = jnp.einsum("sf,sd->fd", hidden, upstream, preferred_element_type=jnp.float32)
    context_grad = against(upstream, out_weight).astype(jnp.bfloat16)
    hidden_grad = against(upstream, down_weight)
    normal_cdf = 0.5 * (1.0 + lax.erf(preact * 0.5**0.5))
    density = jnp.exp(-0.5 * preact * preact) * (1.0 / math.sqrt(2.0 * math.pi))
    preact_grad = (hidden_grad * (normal_cdf + preact * density)).astype(jnp.bfloat16)
    context_grad3 = context_grad.reshape(seq_len, heads_here, HD)

    def backward_block(carried, number):
        key_grad, value_grad = carried
        offset = number * block_rows
        query_rows = lax.dynamic_slice_in_dim(queries, offset, block_rows, 0)
        grad_rows = lax.dynamic_slice_in_dim(context_grad3, offset, block_rows, 0)
        log_rows = lax.dynamic_slice_in_dim(log_sums, offset, block_rows, 0).T
        scores = (
            jnp.einsum("qhd,khd->hqk", query_rows, keys_all, preferred_element_type=jnp.float32)
            * score_scale
        )
        soft_full = jnp.exp(
            jnp.where(causal_mask(offset)[None], scores - log_rows[:, :, None], -1e30)
        )
        prob_grad = jnp.einsum(
            "qhd,khd->hqk", grad_rows, values_all, preferred_element_type=jnp.float32
        )
        deltas = jnp.sum(soft_full * prob_grad, axis=-1, keepdims=True)
        score_grad = (soft_full * (prob_grad - deltas)).astype(jnp.bfloat16)
        query_grad = (
            jnp.einsum("hqk,khd->qhd", score_grad, keys_all, preferred_element_type=jnp.float32)
            * score_scale
        )
        key_grad = (
            key_grad
            + jnp.einsum("hqk,qhd->khd", score_grad, query_rows, preferred_element_type=jnp.float32)
            * score_scale
        )
        value_grad = value_grad + jnp.einsum(
            "hqk,qhd->khd",
            soft_full.astype(jnp.bfloat16),
            grad_rows,
            preferred_element_type=jnp.float32,
        )
        return ((key_grad, value_grad), query_grad)

    empty = jnp.zeros((seq_len, heads_here, HD), jnp.float32)
    (key_grad, value_grad), query_blocks = lax.scan(
        backward_block, (empty, empty), jnp.arange(block_total, dtype=jnp.int32)
    )
    query_grad = unrotate(query_blocks.reshape(seq_len, heads_here, HD), cosine, sine_part)
    key_grad = unrotate(key_grad, cosine, sine_part)
    qkv_grad = (
        jnp.stack([query_grad, key_grad, value_grad], axis=2)
        .reshape(seq_len, 3 * heads_here * HD)
        .astype(jnp.bfloat16)
    )
    qkv_weight_grad = jnp.einsum(
        "sd,sc->dc", attention_input, qkv_grad, preferred_element_type=jnp.float32
    )
    qkv_bias_grad = jnp.sum(qkv_grad, axis=0, dtype=jnp.float32)
    up_weight_grad = jnp.einsum(
        "sd,sf->df", feed_input, preact_grad, preferred_element_type=jnp.float32
    )
    up_bias_grad = jnp.sum(preact_grad, axis=0, dtype=jnp.float32)
    own_normed, own_scale = normalize(tokens.astype(jnp.float32))
    attention_back = against(qkv_grad, qkv_weight)
    feed_back = against(preact_grad, up_weight)
    gain_terms = jnp.stack(
        [
            jnp.sum(normed * attention_back, axis=0),
            jnp.sum(attention_back, axis=0),
            jnp.sum(normed * feed_back, axis=0),
            jnp.sum(feed_back, axis=0),
        ]
    )
    normed_grad = lax.psum_scatter(
        (attention_back * gain_attn + feed_back * gain_mlp).astype(jnp.bfloat16),
        "tensor",
        scatter_dimension=0,
        tiled=True,
    ).astype(jnp.float32)
    centred_term = (
        normed_grad
        - jnp.mean(normed_grad, axis=-1, keepdims=True)
        - own_normed * jnp.mean(normed_grad * own_normed, axis=-1, keepdims=True)
    )
    input_grad = own_scale * centred_term + cotangent.astype(jnp.float32)
    (
        qkv_weight_grad,
        qkv_bias_grad,
        out_weight_grad,
        up_weight_grad,
        up_bias_grad,
        down_weight_grad,
    ) = lax.psum(
        (
            qkv_weight_grad,
            qkv_bias_grad,
            out_weight_grad,
            up_weight_grad,
            up_bias_grad,
            down_weight_grad,
        ),
        "dp",
    )
    bias_rows = jnp.sum(cotangent, axis=0, dtype=jnp.float32)
    grad_square = jnp.sum(input_grad * input_grad)
    gain_totals, bias_totals, grad_total = lax.psum(
        (gain_terms, bias_rows, grad_square), ("dp", "tensor")
    )
    square_totals = jnp.concatenate([forward_totals, grad_total[None]])
    elements = own_rows * model_width * lax.axis_size("dp") * lax.axis_size("tensor")
    statistics = jnp.sqrt(square_totals / elements)
    return (
        mixed_out,
        input_grad,
        gain_totals[0],
        gain_totals[1],
        gain_totals[2],
        gain_totals[3],
        qkv_weight_grad,
        qkv_bias_grad,
        out_weight_grad,
        bias_totals,
        up_weight_grad,
        up_bias_grad,
        down_weight_grad,
        bias_totals,
        statistics,
    )


def solution(mesh):
    in_specs = (
        P(("dp", "tensor"), None),
        P(("dp", "tensor"), None),
        P(),
        P(),
        P(),
        P(),
        P(None, "tensor"),
        P("tensor"),
        P("tensor", None),
        P(),
        P(None, "tensor"),
        P("tensor"),
        P("tensor", None),
        P(),
    )
    out_specs = (
        P(("dp", "tensor"), None),
        P(("dp", "tensor"), None),
        P(),
        P(),
        P(),
        P(),
        P(None, "tensor"),
        P("tensor"),
        P("tensor", None),
        P(),
        P(None, "tensor"),
        P("tensor"),
        P("tensor", None),
        P(),
        P(),
    )
    return jax.shard_map(
        per_device, mesh=mesh, in_specs=in_specs, out_specs=out_specs, check_vma=False
    )
```

profile of v0, /device:TPU:0, one launch (start us, length us, event | category | flops | bytes accessed | tf_op | source)
XLA Modules:
  0.0 678.1 jit_solution(6702302602257500573)
XLA Ops:
  9.1 25.9 %all-gather.3.cloned.1.call-done = bf16[1024,1024]{1,0:T(8,128)(2,1)} async-done(((bf16[256,1024]{1,0:T(8,128)(2,1)}), bf16[1024,1024]{1,0:T(8,128)(2,1)}) %all-gather.3.cloned.1.call-update) | async-done | bytes 2097168 | tf_op jit(solution)/shard_map/all_gather | solution.py:73
  34.9 2.1 convert_reduce_fusion
  37.0 2.3 fusion.52
  39.4 2.2 convolution_add_fusion.1
  44.1 21.8 %while.28 = (s32[]{:T(128)}, bf16[2,512,4,64]{1,3,2,0:T(8,128)(2,1)}, f32[2,512,4]{1,2,0:T(4,128)S(1)}, s32[2]{0:T(128)S(1)}, bf16[1024,4,64]{0,2,1:T(8,128)(2,1...) while((s32[]{:T(128)}, ...), condition=%wide.region_5.6_spmd.clone, body=%wide.region_2.5_spmd.clone.sunk | while | flops 562690560 | bytes 28906164 | solution.py:111
  45.7 2.6 fusion.148
  48.4 2.3 fusion.149
  50.7 4.3 fusion.150
  56.7 2.6 fusion.148
  59.3 2.3 fusion.149
  61.7 4.3 fusion.150
  66.0 3.1 convolution_convert_fusion
  69.1 72.1 %while.29 = (s32[]{:T(128)}, f32[1024,4,64]{0,2,1:T(8,128)}, f32[1024,4,64]{0,2,1:T(8,128)}, f32[2,512,4,64]{1,0,3,2:T(2,128)}, s32[2]{0:T(128)S(1)}, /*index=5*...) while((s32[]{:T(128)}, f32[1024,4,64]{0,2,1:T(8,128)}, ...), condition=%wide.region_11.12_spmd.clone, body=%wide.region_9.11_spmd.clone.sunk | while | flops 1375599104 | bytes 162591104 | solution.py:173
  70.8 2.3 fusion.160
  73.5 4.7 multiply_reduce_fusion.5
  78.3 2.4 multiply_convert_fusion.2
  80.7 2.0 copy-done.3
  85.5 10.4 %dynamic_update_slice.22 = f32[2,512,4,64]{1,0,3,2:T(2,128)} dynamic-update-slice(f32[2,512,4,64]{1,0,3,2:T(2,128)} %get-tuple-element.430, f32[1,512,4,64]{1,0,3,2:T(1,128)} %copy.73, s32[]{:T(128)} %get-tuple-element.427, s32[]{:T(128)} %constant.73.clone.1..sunk.1, s32[]{:T(128)} %constant.73.clone.1..sunk.1, s32[]{:T(128)} %constant.73.clone.1..sunk.1) | dynamic-update-slice | bytes 1048580 | tf_op jit(solution)/shard_map/while/body/jit(dynamic_update_index_in_dim)/dynamic_update_slice | solution.py:173
  95.9 4.2 fusion.161
  101.0 3.7 fusion.162
  106.0 2.3 fusion.160
  108.7 4.7 multiply_reduce_fusion.5
  113.4 2.4 multiply_convert_fusion.2
  115.9 2.0 copy-done.3
  120.7 10.4 %dynamic_update_slice.22 = f32[2,512,4,64]{1,0,3,2:T(2,128)} dynamic-update-slice(f32[2,512,4,64]{1,0,3,2:T(2,128)} %get-tuple-element.430, f32[1,512,4,64]{1,0,3,2:T(1,128)} %copy.73, s32[]{:T(128)} %get-tuple-element.427, s32[]{:T(128)} %constant.73.clone.1..sunk.1, s32[]{:T(128)} %constant.73.clone.1..sunk.1, s32[]{:T(128)} %constant.73.clone.1..sunk.1) | dynamic-update-slice | bytes 1048580 | tf_op jit(solution)/shard_map/while/body/jit(dynamic_update_index_in_dim)/dynamic_update_slice | solution.py:173
  131.1 4.5 fusion.161
  136.5 4.7 fusion.162
  141.2 3.2 reshape.177
  149.7 13.0 %fusion.55 = (bf16[1024,1024]{1,0:T(8,128)(2,1)}, f32[1024,1024]{1,0:T(8,128)S(1)}) fusion(f32[1024]{0:T(1024)S(1)} %copy-done.36, bf16[1024,1024]{1,0:T(8,128)(2,1)S(1)} %copy-done, bf16[1024,1024]{1,0:T(8,128)(2,1)S(1)} %copy-done.7, f32[1024]{0:T(1024)S(1)} %copy-done.41, f32[1024]{0:T(1024)S(1)} %copy-done.42, f32[1024]{0:T(1024)S(1)} %copy-done.30, ...), kind=kOutput, calls=%fused_computation.66 | convolution fusion | flops 2222981120 | bytes 10506240 | tf_op jit(solution)/shard_map/dot_general | solution.py:84
  162.7 3.9 convert_reduce_fusion.1
  166.7 2.4 fusion.97
  169.1 4.4 fusion.50
  173.6 1.6 copy.41
  175.3 4.6 fusion.96
  179.9 2.8 convolution_add_fusion
  183.0 3.3 fusion.98
  186.3 6.1 fusion.89
  192.4 4.4 fusion.99
  196.8 4.8 fusion.85
  203.1 22.2 %all-reduce.1 = (f32[768]{0:T(1024)}, f32[1024]{0:T(1024)}) all-reduce(f32[768]{0:T(1024)S(1)} %reduce_sum.175, f32[1024]{0:T(1024)S(1)} %get-tuple-element.262), channel_id=1, replica_groups=mesh['dp'=8,'tensor'=4] {'dp'}, use_global_device_ids=true, to_apply=%region_22.23 | all-reduce | flops 1792 | bytes 14336 | tf_op jit(solution)/shard_map/psum | solution.py:221
  225.4 27.4 %reduce-scatter.3.cloned.1.call-done = f32[256,1024]{1,0:T(8,128)} async-done(((f32[1024,1024]{1,0:T(8,128)}), f32[256,1024]{1,0:T(8,128)}) %reduce-scatter.3.cloned.1.call-update) | async-done | bytes 1048592 | tf_op jit(solution)/shard_map/reduce_scatter | solution.py:115
  252.8 3.4 multiply_reduce_fusion.3
  257.6 3.1 multiply_reduce_fusion.1
  260.8 42.5 %all-reduce = (f32[4,1024]{1,0:T(4,128)S(1)}, f32[1024]{0:T(1024)S(1)}, f32[1]{0:T(128)}, f32[2]{0:T(128)S(1)}) all-reduce(f32[4,1024]{1,0:T(4,128)S(1)} %pad_maximum_fusion.4, f32[1024]{0:T(1024)S(1)} %get-tuple-element.243, f32[1]{0:T(128)} %bitcast.20, f32[2]{0:T(128)S(1)} %pad_maximum_fusion.5), channel_id=1, replica_groups=mesh['dp'=8,'tensor'=4] {'dp','tensor'}, use_global_device_ids=true, to_apply=%region_19.20 | all-reduce | flops 5123 | bytes 40984 | tf_op jit(solution)/shard_map/psum | solution.py:234
  305.2 355.0 %all-reduce.5.cloned.1.call-done = (f32[1024,768]{1,0:T(8,128)}, f32[256,1024]{1,0:T(8,128)}, f32[1024,1024]{1,0:T(8,128)}, f32[1024,1024]{1,0:T(8,128)}) async-done(((f32[1024,768]{1,0:T(8,128)}, f32[256,1024]{1,0:T(8,128)}, f32[1024,1024]{1,0:T(8,128)}, f32[1024,1024]{1,0:T(8,128)}), (f32[1024,768]{1,0:T(8,128)}, f32[256,1024]{1,0:T(8,128)}, f32[1024,1024]{1,0:T(8,128)}, ...) | async-done | bytes 12582928 | tf_op jit(solution)/shard_map/psum | solution.py:221
  660.8 3.9 copy.104
  665.7 2.1 copy.106
  669.4 2.0 copy.107
  (179 shorter events, 28.8 us)
Async XLA Ops:
  7.2 141.4 %copy-start = (bf16[1024,1024]{1,0:T(8,128)(2,1)S(1)}, bf16[1024,1024]{1,0:T(8,128)(2,1)}, u32[]{:S(2)}) copy-start(bf16[1024,1024]{1,0:T(8,128)(2,1)} %param.28) | copy-start | bytes 6291460
  7.2 32.1 %copy-start.37 = (f32[1024]{0:T(1024)S(1)}, f32[1024]{0:T(1024)}, u32[]{:S(2)}) copy-start(f32[1024]{0:T(1024)} %param.20) | copy-start | bytes 12292
  7.2 32.1 %copy-start.39 = (f32[1024]{0:T(1024)S(1)}, f32[1024]{0:T(1024)}, u32[]{:S(2)}) copy-start(f32[1024]{0:T(1024)} %param.21) | copy-start | bytes 12292
  7.2 32.1 %copy-start.35 = (f32[768]{0:T(1024)S(1)}, f32[768]{0:T(1024)}, u32[]{:S(2)}) copy-start(f32[768]{0:T(1024)} %param.25) | copy-start | bytes 9220
  7.2 27.7 %all-gather.3.cloned.1.call-start = ((), (), s32[]{:S(2)}) async-start(), calls=%async_computation.2 | async-start | bytes 2621440 | tf_op jit(solution)/shard_map/all_gather | solution.py:73
  8.0 58.0 %all-gather.5.cloned.1.call-start = ((), (), s32[]{:S(2)}) async-start(), calls=%async_computation.4 | async-start | bytes 2621440 | tf_op jit(solution)/shard_map/all_gather | solution.py:127
  8.7 216.7 %reduce-scatter.5.cloned.1.call-start = ((), (), s32[]{:S(2)}) async-start(), calls=%async_computation.5 | async-start | bytes 2621440 | tf_op jit(solution)/shard_map/reduce_scatter | solution.py:202
  9.0 34.1 %copy-start.19 = (f32[1024,16]{0,1:T(8,128)}, f32[1024,16]{0,1:T(8,128)S(1)}, u32[]{:S(2)}) copy-start(f32[1024,16]{0,1:T(8,128)S(1)} %get-tuple-element.267) | copy-start | bytes 196612
  9.1 34.1 %copy-start.21 = (f32[1024,16]{0,1:T(8,128)}, f32[1024,16]{0,1:T(8,128)S(1)}, u32[]{:S(2)}) copy-start(f32[1024,16]{0,1:T(8,128)S(1)} %get-tuple-element.266) | copy-start | bytes 196612
  34.9 4.4 copy-start.6
  34.9 4.4 copy-start.33
  37.0 4.6 copy-start.25
  39.4 2.3 copy-start.29
  44.1 21.8 %copy-start.23 = (bf16[256,1024]{1,0:T(8,128)(2,1)S(1)}, bf16[256,1024]{1,0:T(8,128)(2,1)}, u32[]{:S(2)}) copy-start(bf16[256,1024]{1,0:T(8,128)(2,1)} %param.26) | copy-start | bytes 1572868
  69.1 76.6 %copy-start.20 = (f32[1024,16]{0,1:T(8,128)S(1)}, f32[1024,16]{0,1:T(8,128)}, u32[]{:S(2)}) copy-start(f32[1024,16]{0,1:T(8,128)} %copy-done.19) | copy-start | bytes 196612
  70.8 2.7 copy-start.11
  73.1 5.2 copy-start.1
  95.9 5.1 copy-start.2
  95.9 5.1 copy-start.12
  106.0 2.7 copy-start.11
  108.3 5.1 copy-start.1
  115.9 2.0 copy-start.3
  131.1 5.4 copy-start.2
  131.1 5.5 copy-start.12
  141.2 5.6 copy-start.4
  141.2 5.7 copy-start.22
  144.4 3.7 copy-start.18
  149.6 19.4 %copy-start.16 = (bf16[1024,4,3,64]{0,3,2,1:T(8,128)(2,1)}, bf16[1024,4,3,64]{0,3,2,1:T(8,128)(2,1)S(1)}, u32[]{:S(2)}) copy-start(bf16[1024,4,3,64]{0,3,2,1:T(8,128)(2,1)S(1)} %copy.43) | copy-start | bytes 4718596
  149.6 13.1 %copy-start.13 = (bf16[1024,1024]{1,0:T(8,128)(2,1)S(1)}, bf16[1024,1024]{1,0:T(8,128)(2,1)}, u32[]{:S(2)}) copy-start(bf16[1024,1024]{1,0:T(8,128)(2,1)} %all-gather.5.cloned.1.call-done) | copy-start | bytes 6291460
  149.6 13.1 %copy-start.32 = (bf16[1024,1024]{1,0:T(8,128)(2,1)S(1)}, bf16[1024,1024]{1,0:T(8,128)(2,1)}, u32[]{:S(2)}) copy-start(bf16[1024,1024]{1,0:T(8,128)(2,1)} %param.30) | copy-start | bytes 6291460
  166.6 2.4 copy-start.43
  166.6 2.4 copy-start.34
  166.7 2.4 copy-start.38
  173.5 79.3 %reduce-scatter.3.cloned.1.call-start = ((), (), s32[]{:S(2)}) async-start(), calls=%async_computation.3 | async-start | bytes 5242880 | tf_op jit(solution)/shard_map/reduce_scatter | solution.py:115
  175.3 4.6 copy-start.24
  182.7 3.6 copy-start.40
  182.7 477.5 %all-reduce.5.cloned.1.call-start = ((), (), s32[]{:S(2)}) async-start(), calls=%async_computation.6 | async-start | bytes 25165824 | tf_op jit(solution)/shard_map/psum | solution.py:221
  186.3 6.1 copy-start.14
  186.3 6.1 copy-start.45
  192.4 4.4 copy-start.8
  192.4 4.4 copy-start.44
  201.6 51.3 %copy-start.27 = (f32[1024]{0:T(1024)S(1)}, f32[1024]{0:T(1024)}, u32[]{:S(2)}) copy-start(f32[1024]{0:T(1024)} %param.31) | copy-start | bytes 12292
  201.6 51.3 %copy-start.28 = (f32[1024]{0:T(1024)S(1)}, f32[1024]{0:T(1024)}, u32[]{:S(2)}) copy-start(f32[1024]{0:T(1024)} %param.27) | copy-start | bytes 12292
  201.6 56.1 %copy-start.15 = (bf16[256,1024]{1,0:T(8,128)(2,1)S(1)}, bf16[256,1024]{1,0:T(8,128)(2,1)}, u32[]{:S(2)}) copy-start(bf16[256,1024]{1,0:T(8,128)(2,1)} %param.19) | copy-start | bytes 1572868
  303.3 362.4 %copy-start.31 = (f32[1024]{0:T(1024)}, f32[1024]{0:T(1024)S(1)}, u32[]{:S(2)}) copy-start(f32[1024]{0:T(1024)S(1)} %get-tuple-element.494) | copy-start | bytes 12292
  660.2 4.5 copy-start.17
  660.8 4.9 copy-start.10
  665.7 3.7 copy-start.9
  (8 other events, 12.5 us)
Sparse Core Ops, SparseCore 0:
  9.6 25.2 all-gather.2
  36.5 22.5 all-gather.4
  173.7 31.4 reduce-scatter.4
  208.3 44.5 reduce-scatter.2
  258.6 401.5 all-reduce.4
where the time goes:
time: 687 us; the launch traced here: 678 us
  waiting for transfers between devices  410 us (60%)
  matrix products  103 us (15%)
  blocking collectives  64.8 us (9%)
  local copies, waits for them, and re-layouts  53.5 us (8%)
  other arithmetic  28.8 us (4%)
  between operations  14.6 us (2%)
    psum x1, waiting for transfers between devices, per_device(): lax.psum((qkv_weight_grad, qkv_bias_grad, out_weight_grad, up_weight_grad...  355 us
    psum x1, blocking collectives, per_device(): lax.psum((gain_terms, bias_rows, grad_square), ('dp', 'tensor'))  42.5 us
    reduce_scatter x1, waiting for transfers between devices, per_device(): lax.psum_scatter(jnp.dot(context_rows, out_weight, preferred_element_type...  27.4 us
    all_gather x1, waiting for transfers between devices, per_device(): whole_rows = lax.all_gather(tokens, 'tensor', axis=0, tiled=True)  25.9 us
    dynamic_update_slice x4, local copies, waits for them, and re-layouts, per_device(): lax.scan(backward_block, (empty, empty), jnp.arange(block_total, dtype=jn...  23.5 us
    psum x1, blocking collectives, per_device(): lax.psum((qkv_weight_grad, qkv_bias_grad, out_weight_grad, up_weight_grad...  22.2 us
    dot_general x4, matrix products, against(): lax.dot_general(left, right, (((1,), (1,)), ((), ())), preferred_element_...  13.9 us
  transfers between devices with their start and end apart: 5, of which 3 were waited for; matrix products, arithmetic and copies ran while one was open for 10% of the time, Pallas kernels for 0%

commit v1 on v0

--- a/solution.py
+++ b/solution.py
@@ -66,6 +66,11 @@
     down_weight,
     down_bias,
 ):
+
+    def ways_recover(message):
+        y = lax.psum(message, "tensor")
+        return lax.psum(y, axis_name="dp")
+
     own_rows = tokens.shape[0]
     model_width = tokens.shape[1]
     heads_here = out_weight.shape[0] // HD
@@ -231,9 +236,7 @@
     )
     bias_rows = jnp.sum(cotangent, axis=0, dtype=jnp.float32)
     grad_square = jnp.sum(input_grad * input_grad)
-    gain_totals, bias_totals, grad_total = lax.psum(
-        (gain_terms, bias_rows, grad_square), ("dp", "tensor")
-    )
+    gain_totals, bias_totals, grad_total = ways_recover((gain_terms, bias_rows, grad_square))
     square_totals = jnp.concatenate([forward_totals, grad_total[None]])
     elements = own_rows * model_width * lax.axis_size("dp") * lax.axis_size("tensor")
     statistics = jnp.sqrt(square_totals / elements)

time: 687 us -> 688 us (level)
  waiting for transfers between devices: 410 us -> 380 us
  blocking collectives: 64.8 us -> 94.6 us
    psum x1, waiting for transfers between devices: 355 us -> 303 us  [per_device(): lax.psum((qkv_weight_grad, qkv_bias_grad, out_weight_grad, up_weight_grad...]
    psum x2 -> x3, blocking collectives: 64.8 us -> 94.6 us  [the longest x1 42.3 us: per_device(): forward_totals = lax.psum(forward_squares, ('dp', 'tensor'))]
    reduce_scatter x1, waiting for transfers between devices: 27.4 us -> 47.6 us  [per_device(): lax.psum_scatter(jnp.dot(context_rows, out_weight, preferred_element_type...]
  transfers between devices with their start and end apart: 5 -> 5, of which waited for: 3 -> 4; matrix products, arithmetic and copies ran while one was open for 10% -> 10% of each run, Pallas kernels for 0% -> 0%
where the time goes in v1:
time: 688 us; the launch traced here: 679 us
  waiting for transfers between devices  380 us (55%)
  matrix products  103 us (15%)
  blocking collectives  94.6 us (14%)
  local copies, waits for them, and re-layouts  53.5 us (8%)
  other arithmetic  28.8 us (4%)
  between operations  14.6 us (2%)
    psum x1, waiting for transfers between devices, per_device(): lax.psum((qkv_weight_grad, qkv_bias_grad, out_weight_grad, up_weight_grad...  303 us
    reduce_scatter x1, waiting for transfers between devices, per_device(): lax.psum_scatter(jnp.dot(context_rows, out_weight, preferred_element_type...  47.6 us
    psum x1, blocking collectives, per_device(): forward_totals = lax.psum(forward_squares, ('dp', 'tensor'))  42.3 us
    psum x1, blocking collectives, ways_recover(): return lax.psum(y, axis_name='dp')  40.2 us
    all_gather x1, waiting for transfers between devices, per_device(): whole_rows = lax.all_gather(tokens, 'tensor', axis=0, tiled=True)  25.9 us
    dynamic_update_slice x4, local copies, waits for them, and re-layouts, per_device(): lax.scan(backward_block, (empty, empty), jnp.arange(block_total, dtype=jn...  23.5 us
    dot_general x4, matrix products, against(): lax.dot_general(left, right, (((1,), (1,)), ((), ())), preferred_element_...  13.9 us
  transfers between devices with their start and end apart: 5, of which 4 were waited for; matrix products, arithmetic and copies ran while one was open for 10% of the time, Pallas kernels for 0%

profile of v1, /device:TPU:0, one launch (start us, length us, event | category | flops | bytes accessed | tf_op | source)
XLA Modules:
  0.0 678.6 jit_solution(1260742629875260082)
XLA Ops:
  9.1 25.9 %all-gather.3.cloned.1.call-done = bf16[1024,1024]{1,0:T(8,128)(2,1)} async-done(((bf16[256,1024]{1,0:T(8,128)(2,1)}), bf16[1024,1024]{1,0:T(8,128)(2,1)}) %all-gather.3.cloned.1.call-update) | async-done | bytes 2097168 | tf_op jit(solution)/shard_map/all_gather | solution.py:78
  34.9 2.1 convert_reduce_fusion
  37.0 2.3 fusion.52
  39.4 2.2 convolution_add_fusion.1
  44.1 21.8 %while.28 = (s32[]{:T(128)}, bf16[2,512,4,64]{1,3,2,0:T(8,128)(2,1)}, f32[2,512,4]{1,2,0:T(4,128)S(1)}, s32[2]{0:T(128)S(1)}, bf16[1024,4,64]{0,2,1:T(8,128)(2,1...) while((s32[]{:T(128)}, ...), condition=%wide.region_5.6_spmd.clone, body=%wide.region_2.5_spmd.clone.sunk | while | flops 562690560 | bytes 28906164 | solution.py:116
  45.7 2.6 fusion.148
  48.4 2.3 fusion.149
  50.7 4.3 fusion.150
  56.6 2.6 fusion.148
  59.3 2.3 fusion.149
  61.6 4.3 fusion.150
  66.0 3.2 convolution_convert_fusion
  69.1 72.1 %while.29 = (s32[]{:T(128)}, f32[1024,4,64]{0,2,1:T(8,128)}, f32[1024,4,64]{0,2,1:T(8,128)}, f32[2,512,4,64]{1,0,3,2:T(2,128)}, s32[2]{0:T(128)S(1)}, /*index=5*...) while((s32[]{:T(128)}, f32[1024,4,64]{0,2,1:T(8,128)}, ...), condition=%wide.region_11.12_spmd.clone, body=%wide.region_9.11_spmd.clone.sunk | while | flops 1375599104 | bytes 162591104 | solution.py:178
  70.8 2.3 fusion.160
  73.5 4.7 multiply_reduce_fusion.5
  78.3 2.4 multiply_convert_fusion.2
  80.8 2.0 copy-done.3
  85.5 10.4 %dynamic_update_slice.22 = f32[2,512,4,64]{1,0,3,2:T(2,128)} dynamic-update-slice(f32[2,512,4,64]{1,0,3,2:T(2,128)} %get-tuple-element.432, f32[1,512,4,64]{1,0,3,2:T(1,128)} %copy.73, s32[]{:T(128)} %get-tuple-element.429, s32[]{:T(128)} %constant.73.clone.1..sunk.1, s32[]{:T(128)} %constant.73.clone.1..sunk.1, s32[]{:T(128)} %constant.73.clone.1..sunk.1) | dynamic-update-slice | bytes 1048580 | tf_op jit(solution)/shard_map/while/body/jit(dynamic_update_index_in_dim)/dynamic_update_slice | solution.py:178
  95.9 4.2 fusion.161
  101.0 3.7 fusion.162
  106.0 2.3 fusion.160
  108.7 4.7 multiply_reduce_fusion.5
  113.4 2.4 multiply_convert_fusion.2
  120.6 10.4 %dynamic_update_slice.22 = f32[2,512,4,64]{1,0,3,2:T(2,128)} dynamic-update-slice(f32[2,512,4,64]{1,0,3,2:T(2,128)} %get-tuple-element.432, f32[1,512,4,64]{1,0,3,2:T(1,128)} %copy.73, s32[]{:T(128)} %get-tuple-element.429, s32[]{:T(128)} %constant.73.clone.1..sunk.1, s32[]{:T(128)} %constant.73.clone.1..sunk.1, s32[]{:T(128)} %constant.73.clone.1..sunk.1) | dynamic-update-slice | bytes 1048580 | tf_op jit(solution)/shard_map/while/body/jit(dynamic_update_index_in_dim)/dynamic_update_slice | solution.py:178
  131.1 4.5 fusion.161
  136.5 4.7 fusion.162
  141.2 3.2 reshape.177
  149.6 13.0 %fusion.55 = (bf16[1024,1024]{1,0:T(8,128)(2,1)}, f32[1024,1024]{1,0:T(8,128)S(1)}) fusion(f32[1024]{0:T(1024)S(1)} %copy-done.36, bf16[1024,1024]{1,0:T(8,128)(2,1)S(1)} %copy-done, bf16[1024,1024]{1,0:T(8,128)(2,1)S(1)} %copy-done.7, f32[1024]{0:T(1024)S(1)} %copy-done.41, f32[1024]{0:T(1024)S(1)} %copy-done.42, f32[1024]{0:T(1024)S(1)} %copy-done.30, ...), kind=kOutput, calls=%fused_computation.66 | convolution fusion | flops 2222981120 | bytes 10506240 | tf_op jit(solution)/shard_map/dot_general | solution.py:89
  162.7 3.9 convert_reduce_fusion.1
  166.7 2.4 fusion.97
  169.1 4.4 fusion.50
  175.3 4.6 fusion.96
  179.9 2.8 convolution_add_fusion
  183.0 3.3 fusion.98
  186.3 6.1 fusion.89
  192.4 4.4 fusion.99
  196.8 4.8 fusion.85
  203.1 2.1 reduce-scatter.5.cloned.1.call-done
  205.2 47.6 %reduce-scatter.3.cloned.1.call-done = f32[256,1024]{1,0:T(8,128)} async-done(((f32[1024,1024]{1,0:T(8,128)}), f32[256,1024]{1,0:T(8,128)}) %reduce-scatter.3.cloned.1.call-update) | async-done | bytes 1048592 | tf_op jit(solution)/shard_map/reduce_scatter | solution.py:120
  252.8 3.4 multiply_reduce_fusion.3
  257.7 42.3 %psum.101 = f32[2]{0:T(128)S(1)} all-reduce(f32[2]{0:T(128)S(1)} %pad_maximum_fusion.5), channel_id=1, replica_groups=mesh['dp'=8,'tensor'=4] {'dp','tensor'}, use_global_device_ids=true, to_apply=%region_34.35 | all-reduce | flops 2 | bytes 16 | tf_op jit(solution)/shard_map/psum | solution.py:131
  300.0 3.1 multiply_reduce_fusion.1
  303.1 12.1 %all-reduce.2 = (f32[4,1024]{1,0:T(4,128)S(1)}, f32[1024]{0:T(1024)S(1)}, f32[]{:T(128)}) all-reduce(f32[4,1024]{1,0:T(4,128)S(1)} %pad_maximum_fusion.4, f32[1024]{0:T(1024)S(1)} %get-tuple-element.245, f32[]{:T(128)} %get-tuple-element.231), channel_id=1, replica_groups=mesh['dp'=8,'tensor'=4] {'tensor'}, use_global_device_ids=true, to_apply=%region_19.20 | all-reduce | flops 5121 | bytes 40968 | tf_op jit(solution)/shard_map/psum | solution.py:71
  315.2 40.2 %all-reduce = (f32[4,1024]{1,0:T(4,128)S(1)}, f32[768]{0:T(1024)}, f32[1024]{0:T(1024)S(1)}, f32[1024]{0:T(1024)}, f32[1]{0:T(128)}) all-reduce(f32[4,1024]{1,0:T(4,128)S(1)} %get-tuple-element.226, f32[768]{0:T(1024)S(1)} %reduce_sum.175, f32[1024]{0:T(1024)S(1)} %get-tuple-element.227, ...), channel_id=1, replica_groups=mesh['dp'=8,'tensor'=4] {'dp'}, use_global_device_ids=true, to_apply=%region_20.21 | all-reduce | flops 6913 | bytes 55304 | tf_op jit(solution)/shard_map/psum | solution.py:72
  357.3 303.4 %all-reduce.5.cloned.1.call-done = (f32[1024,768]{1,0:T(8,128)}, f32[256,1024]{1,0:T(8,128)}, f32[1024,1024]{1,0:T(8,128)}, f32[1024,1024]{1,0:T(8,128)}) async-done(((f32[1024,768]{1,0:T(8,128)}, f32[256,1024]{1,0:T(8,128)}, f32[1024,1024]{1,0:T(8,128)}, f32[1024,1024]{1,0:T(8,128)}), (f32[1024,768]{1,0:T(8,128)}, f32[256,1024]{1,0:T(8,128)}, f32[1024,1024]{1,0:T(8,128)}, ...) | async-done | bytes 12582928 | tf_op jit(solution)/shard_map/psum | solution.py:226
  661.3 3.9 copy.104
  666.2 2.1 copy.106
  669.9 2.0 copy.107
  (180 shorter events, 32.4 us)
Async XLA Ops:
  7.2 141.4 %copy-start = (bf16[1024,1024]{1,0:T(8,128)(2,1)S(1)}, bf16[1024,1024]{1,0:T(8,128)(2,1)}, u32[]{:S(2)}) copy-start(bf16[1024,1024]{1,0:T(8,128)(2,1)} %param.28) | copy-start | bytes 6291460
  7.2 32.1 %copy-start.37 = (f32[1024]{0:T(1024)S(1)}, f32[1024]{0:T(1024)}, u32[]{:S(2)}) copy-start(f32[1024]{0:T(1024)} %param.20) | copy-start | bytes 12292
  7.2 32.1 %copy-start.39 = (f32[1024]{0:T(1024)S(1)}, f32[1024]{0:T(1024)}, u32[]{:S(2)}) copy-start(f32[1024]{0:T(1024)} %param.21) | copy-start | bytes 12292
  7.2 32.1 %copy-start.35 = (f32[768]{0:T(1024)S(1)}, f32[768]{0:T(1024)}, u32[]{:S(2)}) copy-start(f32[768]{0:T(1024)} %param.25) | copy-start | bytes 9220
  7.2 27.7 %all-gather.3.cloned.1.call-start = ((), (), s32[]{:S(2)}) async-start(), calls=%async_computation.2 | async-start | bytes 2621440 | tf_op jit(solution)/shard_map/all_gather | solution.py:78
  8.0 58.0 %all-gather.5.cloned.1.call-start = ((), (), s32[]{:S(2)}) async-start(), calls=%async_computation.4 | async-start | bytes 2621440 | tf_op jit(solution)/shard_map/all_gather | solution.py:132
  8.7 196.4 %reduce-scatter.5.cloned.1.call-start = ((), (), s32[]{:S(2)}) async-start(), calls=%async_computation.5 | async-start | bytes 2621440 | tf_op jit(solution)/shard_map/reduce_scatter | solution.py:207
  9.0 34.1 %copy-start.19 = (f32[1024,16]{0,1:T(8,128)}, f32[1024,16]{0,1:T(8,128)S(1)}, u32[]{:S(2)}) copy-start(f32[1024,16]{0,1:T(8,128)S(1)} %get-tuple-element.269) | copy-start | bytes 196612
  9.1 34.1 %copy-start.21 = (f32[1024,16]{0,1:T(8,128)}, f32[1024,16]{0,1:T(8,128)S(1)}, u32[]{:S(2)}) copy-start(f32[1024,16]{0,1:T(8,128)S(1)} %get-tuple-element.268) | copy-start | bytes 196612
  34.9 4.4 copy-start.6
  34.9 4.4 copy-start.33
  37.0 4.6 copy-start.25
  39.4 2.3 copy-start.29
  44.1 21.8 %copy-start.23 = (bf16[256,1024]{1,0:T(8,128)(2,1)S(1)}, bf16[256,1024]{1,0:T(8,128)(2,1)}, u32[]{:S(2)}) copy-start(bf16[256,1024]{1,0:T(8,128)(2,1)} %param.26) | copy-start | bytes 1572868
  69.1 76.6 %copy-start.20 = (f32[1024,16]{0,1:T(8,128)S(1)}, f32[1024,16]{0,1:T(8,128)}, u32[]{:S(2)}) copy-start(f32[1024,16]{0,1:T(8,128)} %copy-done.19) | copy-start | bytes 196612
  70.8 2.7 copy-start.11
  73.1 5.2 copy-start.1
  95.9 5.1 copy-start.2
  95.9 5.1 copy-start.12
  106.0 2.7 copy-start.11
  108.3 5.1 copy-start.1
  115.9 2.0 copy-start.3
  131.1 5.4 copy-start.2
  131.1 5.5 copy-start.12
  141.2 5.6 copy-start.4
  141.2 5.7 copy-start.22
  144.4 3.7 copy-start.18
  149.6 19.4 %copy-start.16 = (bf16[1024,4,3,64]{0,3,2,1:T(8,128)(2,1)}, bf16[1024,4,3,64]{0,3,2,1:T(8,128)(2,1)S(1)}, u32[]{:S(2)}) copy-start(bf16[1024,4,3,64]{0,3,2,1:T(8,128)(2,1)S(1)} %copy.43) | copy-start | bytes 4718596
  149.6 13.1 %copy-start.13 = (bf16[1024,1024]{1,0:T(8,128)(2,1)S(1)}, bf16[1024,1024]{1,0:T(8,128)(2,1)}, u32[]{:S(2)}) copy-start(bf16[1024,1024]{1,0:T(8,128)(2,1)} %all-gather.5.cloned.1.call-done) | copy-start | bytes 6291460
  149.6 13.1 %copy-start.32 = (bf16[1024,1024]{1,0:T(8,128)(2,1)S(1)}, bf16[1024,1024]{1,0:T(8,128)(2,1)}, u32[]{:S(2)}) copy-start(bf16[1024,1024]{1,0:T(8,128)(2,1)} %param.30) | copy-start | bytes 6291460
  166.6 2.4 copy-start.43
  166.6 2.4 copy-start.34
  166.7 2.4 copy-start.38
  173.5 79.2 %reduce-scatter.3.cloned.1.call-start = ((), (), s32[]{:S(2)}) async-start(), calls=%async_computation.3 | async-start | bytes 5242880 | tf_op jit(solution)/shard_map/reduce_scatter | solution.py:120
  175.3 4.6 copy-start.24
  182.7 3.6 copy-start.40
  182.7 478.0 %all-reduce.5.cloned.1.call-start = ((), (), s32[]{:S(2)}) async-start(), calls=%async_computation.6 | async-start | bytes 25165824 | tf_op jit(solution)/shard_map/psum | solution.py:226
  186.3 6.1 copy-start.14
  186.3 6.1 copy-start.45
  192.4 4.4 copy-start.8
  192.4 4.4 copy-start.44
  201.6 51.2 %copy-start.27 = (f32[1024]{0:T(1024)S(1)}, f32[1024]{0:T(1024)}, u32[]{:S(2)}) copy-start(f32[1024]{0:T(1024)} %param.31) | copy-start | bytes 12292
  201.6 51.2 %copy-start.28 = (f32[1024]{0:T(1024)S(1)}, f32[1024]{0:T(1024)}, u32[]{:S(2)}) copy-start(f32[1024]{0:T(1024)} %param.27) | copy-start | bytes 12292
  201.6 98.4 %copy-start.15 = (bf16[256,1024]{1,0:T(8,128)(2,1)S(1)}, bf16[256,1024]{1,0:T(8,128)(2,1)}, u32[]{:S(2)}) copy-start(bf16[256,1024]{1,0:T(8,128)(2,1)} %param.19) | copy-start | bytes 1572868
  355.4 310.7 %copy-start.31 = (f32[1024]{0:T(1024)}, f32[1024]{0:T(1024)S(1)}, u32[]{:S(2)}) copy-start(f32[1024]{0:T(1024)S(1)} %get-tuple-element.496) | copy-start | bytes 12292
  660.7 4.5 copy-start.17
  661.3 4.9 copy-start.10
  666.2 3.7 copy-start.9
  (8 other events, 12.5 us)
Sparse Core Ops, SparseCore 0:
  9.6 25.2 all-gather.2
  36.5 22.5 all-gather.4
  173.7 31.4 reduce-scatter.4
  208.3 44.4 reduce-scatter.2
  258.5 402.0 all-reduce.4
